TPU v7x, 256 devices: a whole 4x4x8 slice. The times are simulated.
256 devices in a mesh: tile: 8 (over y, core), freq: 32 (over x, z).
Axes of the slice: x: 4, y: 4, z: 8, core: 2. Of those that a mesh axis runs over, the one named last changes fastest.
Arguments:
- sensitivity: float32 [8, 32, 2, 1024, 512], P('tile', 'freq'), may hold values from -0.25 to 0.25
- models: float32 [2048, 256], P(('tile', 'freq')), may hold values from -6 to 6
- observed: float32 [8, 40, 1024], P('tile', None, 'freq'), may hold values from -6 to 6
- waveform: float32 [128], replicated, may hold values from -0.5 to 0.5
- cell_index: int32 [8, 512], P('tile'), may hold values from 0 to 2047, as said below
- gate_index: int32 [40], replicated, may hold values from 10 to 127, as said below
Outputs:
- updated: float32 [2048, 256], P(('tile', 'freq'))
- misfit: float32 [256], replicated
Inputs may be any that keep to these rules, and one draw needn't show every extreme that they name: `cell_index`: each tile's indices are distinct. Tile t holds, in some order, the 256 global cells from t * 256 on and the 256 cells of one other tile's block (from u * 256 on, u != t). Every global cell belongs to one or more tiles. `gate_index`: strictly increasing; the last gate is sample 128 - 1.
All inputs are finite; a program needn't handle non-finite values.
Results may differ from a plain program's by a relative error of at most 0.00017.
Values sent between devices are 32-bit elements; how exact they have to be, the bound alone decides.
A program may use at most 64 MiB of HBM per device.

v0:
```python
import math
import jax
import jax.numpy as jnp
from jax import lax
from jax.sharding import PartitionSpec as P

HIGH = lax.Precision.HIGHEST
PHASE_RATE = 0.37
STEP_LENGTH = 0.5
EPSILON = 1e-06


def gate_tables(freqs, waveform, gate_index):
    samples = waveform.shape[0]
    freq_col = jnp.arange(freqs, dtype=jnp.float32)[:, None] + 0.5
    time_row = jnp.arange(samples, dtype=jnp.float32)[None, :] + 0.5
    phases = PHASE_RATE * freq_col * time_row
    kernel = jnp.stack([jnp.cos(phases), jnp.sin(phases)], axis=1) / math.sqrt(freqs)
    time_lag = jnp.arange(samples)[:, None] - jnp.arange(samples)[None, :]
    toeplitz = jnp.where(time_lag >= 0, jnp.take(waveform, jnp.clip(time_lag, 0, samples - 1)), 0.0)
    picker = (gate_index[:, None] == jnp.arange(samples)[None, :]).astype(jnp.float32)
    return (kernel, toeplitz, picker)


def body(sensitivity, models, observed, waveform, cell_index, gate_index):
    freqs = sensitivity.shape[1] * lax.axis_size("freq")
    soundings = sensitivity.shape[3]
    members = models.shape[1]
    gates = gate_index.shape[0]
    devices = lax.axis_size(("tile", "freq"))
    owned_count = models.shape[0]
    ncells = owned_count * devices
    total = lax.axis_size("tile") * soundings * gates
    kernel, toeplitz, picker = gate_tables(freqs, waveform, gate_index)
    block = sensitivity[0]
    all_models = lax.all_gather(models, ("tile", "freq"), axis=0, tiled=True)
    tile_cells = cell_index[0]
    tile_models = jnp.take(all_models, tile_cells, axis=0)
    predicted = jnp.einsum("fpsc,cm->fpsm", block, tile_models, precision=HIGH)
    spectra = lax.all_to_all(predicted, "freq", split_axis=2, concat_axis=0, tiled=True)
    series = jnp.einsum("fpk,fpsm->ksm", kernel, spectra, precision=HIGH)
    series = jnp.einsum("kj,jsm->ksm", toeplitz, series, precision=HIGH)
    response = jnp.einsum("gk,ksm->gsm", picker, series, precision=HIGH)
    misfit_rows = response - observed[0][:, :, None]
    partial_misfit = jnp.sum(misfit_rows * misfit_rows, axis=(0, 1))
    misfit_total = lax.psum(partial_misfit, ("tile", "freq"))
    upward = jnp.einsum("gk,gsm->ksm", picker, misfit_rows, precision=HIGH)
    upward = jnp.einsum("kj,ksm->jsm", toeplitz, upward, precision=HIGH)
    back = jnp.einsum("fpk,ksm->fpsm", kernel, upward, precision=HIGH)
    back_spectra = lax.all_to_all(back, "freq", split_axis=0, concat_axis=2, tiled=True)
    cell_terms = jnp.einsum("fpsc,fpsm->cm", block, back_spectra, precision=HIGH)
    scattered = jnp.zeros((ncells, members), jnp.float32).at[tile_cells].add(cell_terms)
    summed = lax.psum(scattered, ("tile", "freq"))
    gradient = lax.dynamic_slice_in_dim(
        summed, lax.axis_index(("tile", "freq")) * owned_count, owned_count, 0
    )
    partial_square = jnp.sum(gradient * gradient, axis=0)
    square_total = lax.psum(partial_square, ("tile", "freq"))
    misfit = misfit_total / (2.0 * total)
    scale = jnp.sqrt(square_total / ncells + EPSILON)
    updated = models - STEP_LENGTH * (misfit / scale)[None, :] * gradient
    return (updated, misfit)


def solution(mesh):
    in_specs = (
        P("tile", "freq", None, None, None),
        P(("tile", "freq"), None),
        P("tile", None, "freq"),
        P(),
        P("tile", None),
        P(),
    )
    out_specs = (P(("tile", "freq"), None), P())
    return jax.shard_map(body, mesh=mesh, in_specs=in_specs, out_specs=out_specs, check_vma=False)
```

profile of v0, /device:TPU:1, one launch (start us, length us, event | category | flops | bytes accessed | tf_op | source)
XLA Modules:
  0.0 677.4 jit_solution(5995075499652823662)
XLA Ops:
  7.2 0.0 copy-start
  7.2 0.0 all-gather.2.cloned.1.call-start
  7.2 0.7 all-gather.2.cloned.1.call-update
  7.9 0.7 compare_select_fusion.2
  8.6 0.7 compare_and_fusion
  9.3 110.7 %all-gather.2.cloned.1.call-done = f32[2048,256]{1,0:T(8,128)} async-done(((f32[8,256]{1,0:T(8,128)}), f32[2048,256]{1,0:T(8,128)}) %all-gather.2.cloned.1.call-update) | async-done | bytes 2097168 | tf_op jit(solution)/shard_map/all_gather | solution.py:36
  120.0 3.2 gather_fusion.1
  123.2 9.0 %fusion.11 = f32[1,2,1024,256]{2,3,1,0:T(8,128)S(1)} fusion(f32[1,1,2,1024,512]{4,3,2,1,0:T(8,128)} %param.6, f32[512,256]{1,0:T(8,128)S(1)} %gather_fusion.1, pred[512]{0:T(512)(128)(4,1)S(1)} %compare_and_fusion), kind=kOutput, calls=%fused_computation.14 | convolution fusion | flops 3221356544 | bytes 6816256 | tf_op jit(solution)/shard_map/fpsc,cm->fpsm/dot_general | solution.py:39
  132.2 2.4 copy.25
  134.6 7.4 %all-to-all-start = ((f32[1,2,1024,256]{3,1,0,2:T(2,128)}), f32[1,2,1024,256]{3,1,0,2:T(2,128)S(1)}, u32[]{:S(2)}, u32[]{:S(2)}) async-start(f32[1,2,1024,256]{3,1,0,2:T(2,128)} %copy.25), calls=%async_computation | async-start | bytes 4194304 | tf_op jit(solution)/shard_map/all_to_all | solution.py:40
  142.0 0.0 all-reduce.3.cloned.1.call-start
  142.1 0.0 copy-done
  142.1 97.4 %gather_fusion = f32[16384]{0:T(1024)S(1)} fusion(f32[128]{0:T(128)S(1)} %copy-done, s32[16384]{0:T(1024)S(1)} %fusion.24), kind=kCustom, calls=%fused_computation | custom fusion | bytes 196608 | tf_op jit(solution)/shard_map/jit(_take)/gather | solution.py:20
  239.5 0.1 multiply_cosine_fusion
  239.6 0.0 all-to-all-done
  239.7 4.7 fusion.8
  244.3 0.0 copy-start.3
  244.3 0.0 copy-start.4
  244.3 4.0 fusion.2
  248.4 0.0 copy-done.3
  248.4 0.0 copy-done.4
  248.4 1.9 multiply_reduce_fusion
  250.3 1.9 fusion.38
  252.2 4.3 fusion.25
  256.5 2.3 fusion
  258.8 1.2 copy.29
  260.1 56.3 %all_to_all.33 = f32[32,2,32,256]{3,2,1,0:T(8,128)S(1)} all-to-all(f32[32,2,32,256]{3,2,1,0:T(8,128)S(1)} %copy.29), channel_id=1, replica_groups=mesh['tile'=8,'freq'=32] {'freq'}, dimensions={0} | all-to-all | bytes 4194304 | tf_op jit(solution)/shard_map/all_to_all | solution.py:50
  316.3 0.0 copy-start.1
  316.3 0.2 copy.30
  316.6 1.9 copy-done.1
  318.5 3.8 fusion.14
  322.4 0.2 copy.32
  322.6 0.0 copy-start.2
  322.6 4.7 scatter_custom_fusion
  327.3 0.0 all-reduce.3.cloned.1.call-update
  327.3 263.0 %all-reduce.3.cloned.1.call-done = f32[2048,256]{1,0:T(8,128)} async-done(((f32[2048,256]{1,0:T(8,128)}), f32[2048,256]{1,0:T(8,128)}) %all-reduce.3.cloned.1.call-update) | async-done | bytes 2097168 | tf_op jit(solution)/shard_map/psum | solution.py:53
  590.3 0.7 multiply_reduce_fusion.1
  591.0 77.7 %all-reduce = (f32[256]{0:T(256)S(1)}, f32[256]{0:T(256)S(1)}) all-reduce(f32[256]{0:T(256)S(1)} %get-tuple-element.8, f32[256]{0:T(256)S(1)} %multiply_reduce_fusion.1), channel_id=1, replica_groups=mesh['tile'=8,'freq'=32] {'tile','freq'}, use_global_device_ids=true, to_apply=%region_1.2 | all-reduce | flops 512 | bytes 4096 | tf_op jit(solution)/shard_map/psum | solution.py:46
  668.7 0.6 multiply_multiply_fusion
  669.3 0.0 copy-done.2
  669.3 1.3 multiply_subtract_fusion
  (4 shorter events, 0.1 us)
Async XLA Ops:
  7.2 134.9 %copy-start = (f32[128]{0:T(128)S(1)}, f32[128]{0:T(128)}, u32[]{:S(2)}) copy-start(f32[128]{0:T(128)} %param.9) | copy-start | bytes 1540
  7.2 112.9 %all-gather.2.cloned.1.call-start = ((), (), s32[]{:S(2)}) async-start(), calls=%async_computation.2 | async-start | bytes 2105344 | tf_op jit(solution)/shard_map/all_gather | solution.py:36
  134.6 105.1 %all-to-all-start = ((f32[1,2,1024,256]{3,1,0,2:T(2,128)}), f32[1,2,1024,256]{3,1,0,2:T(2,128)S(1)}, u32[]{:S(2)}, u32[]{:S(2)}) async-start(f32[1,2,1024,256]{3,1,0,2:T(2,128)} %copy.25), calls=%async_computation | async-start | bytes 4194304 | tf_op jit(solution)/shard_map/all_to_all | solution.py:40
  142.0 448.3 %all-reduce.3.cloned.1.call-start = ((), (), s32[]{:S(2)}) async-start(), calls=%async_computation.3 | async-start | bytes 4194304 | tf_op jit(solution)/shard_map/psum | solution.py:53
  244.3 4.1 copy-start.3
  244.3 4.1 copy-start.4
  316.3 2.2 copy-start.1
  322.6 346.7 %copy-start.2 = (f32[8,256]{1,0:T(8,128)S(1)}, f32[8,256]{1,0:T(8,128)}, u32[]{:S(2)}) copy-start(f32[8,256]{1,0:T(8,128)} %param.7) | copy-start | bytes 24580
Sparse Core Ops, SparseCore 0:
  11.7 108.2 all-gather.1
  327.4 262.8 all-reduce.2
where the time goes:
time: 678 us; the launch traced here: 677 us
  waiting for transfers between devices  374 us (55%)
  blocking collectives  134 us (20%)
  local copies, waits for them, and re-layouts  107 us (16%)
  matrix products  31.9 us (5%)
  between operations  14.2 us (2%)
  other arithmetic  8.85 us (1%)
  starting transfers between devices  7.46 us (1%)
    psum x1, waiting for transfers between devices, body(): summed = lax.psum(scattered, ('tile', 'freq'))  263 us
    all_gather x1, waiting for transfers between devices, body(): all_models = lax.all_gather(models, ('tile', 'freq'), axis=0, tiled=True)  111 us
    gather x1, local copies, waits for them, and re-layouts, gate_tables(): jnp.take(waveform, jnp.clip(time_lag, 0, samples - 1))  97.4 us
    psum x1, blocking collectives, body(): misfit_total = lax.psum(partial_misfit, ('tile', 'freq'))  77.7 us
    all_to_all x1, blocking collectives, body(): lax.all_to_all(back, 'freq', split_axis=0, concat_axis=2, tiled=True)  56.3 us
  transfers between devices with their start and end apart: 3, of which 2 were waited for; matrix products, arithmetic and copies ran while one was open for 15% of the time, Pallas kernels for 0%

commit v1 on v0

--- a/solution.py
+++ b/solution.py
@@ -50,7 +50,7 @@
     back_spectra = lax.all_to_all(back, "freq", split_axis=0, concat_axis=2, tiled=True)
     cell_terms = jnp.einsum("fpsc,fpsm->cm", block, back_spectra, precision=HIGH)
     scattered = jnp.zeros((ncells, members), jnp.float32).at[tile_cells].add(cell_terms)
-    summed = lax.psum(scattered, ("tile", "freq"))
+    summed = lax.psum(lax.psum(scattered, "freq"), "tile")
     gradient = lax.dynamic_slice_in_dim(
         summed, lax.axis_index(("tile", "freq")) * owned_count, owned_count, 0
     )

time: 678 us -> 639 us (0.942)
  waiting for transfers between devices: 374 us -> 335 us
    psum x1 -> x2, waiting for transfers between devices: 263 us -> 224 us  [body(): summed = lax.psum(lax.psum(scattered, 'freq'), 'tile')]
  transfers between devices with their start and end apart: 3 -> 4, of which waited for: 2 -> 3; matrix products, arithmetic and copies ran while one was open for 15% -> 15% of each run, Pallas kernels for 0% -> 0%
where the time goes in v1:
time: 639 us
  waiting for transfers between devices  335 us (52%)
  blocking collectives  135 us (21%)
  local copies, waits for them, and re-layouts  107 us (17%)
  matrix products  31.9 us (5%)
  between operations  13.9 us (2%)
  other arithmetic  8.85 us (1%)
  starting transfers between devices  7.5 us (1%)
    psum x2, waiting for transfers between devices, body(): summed = lax.psum(lax.psum(scattered, 'freq'), 'tile')  224 us
    all_gather x1, waiting for transfers between devices, body(): all_models = lax.all_gather(models, ('tile', 'freq'), axis=0, tiled=True)  111 us
    gather x1, local copies, waits for them, and re-layouts, gate_tables(): jnp.take(waveform, jnp.clip(time_lag, 0, samples - 1))  97.4 us
    psum x1, blocking collectives, body(): misfit_total = lax.psum(partial_misfit, ('tile', 'freq'))  78.6 us
    all_to_all x1, blocking collectives, body(): lax.all_to_all(back, 'freq', split_axis=0, concat_axis=2, tiled=True)  56.3 us
  transfers between devices with their start and end apart: 4, of which 3 were waited for; matrix products, arithmetic and copies ran while one was open for 15% of the time, Pallas kernels for 0%

profile of v1, /device:TPU:1, one launch (start us, length us, event | category | flops | bytes accessed | tf_op | source)
XLA Modules:
  0.0 638.7 jit_solution(1573145738057989434)
XLA Ops:
  7.2 0.0 copy-start
  7.2 0.0 all-gather.2.cloned.1.call-start
  7.2 0.7 all-gather.2.cloned.1.call-update
  7.9 0.7 compare_select_fusion.2
  8.6 0.7 compare_and_fusion
  9.3 110.7 %all-gather.2.cloned.1.call-done = f32[2048,256]{1,0:T(8,128)} async-done(((f32[8,256]{1,0:T(8,128)}), f32[2048,256]{1,0:T(8,128)}) %all-gather.2.cloned.1.call-update) | async-done | bytes 2097168 | tf_op jit(solution)/shard_map/all_gather | solution.py:36
  120.0 3.2 gather_fusion.1
  123.2 9.0 %fusion.11 = f32[1,2,1024,256]{2,3,1,0:T(8,128)S(1)} fusion(f32[1,1,2,1024,512]{4,3,2,1,0:T(8,128)} %param.6, f32[512,256]{1,0:T(8,128)S(1)} %gather_fusion.1, pred[512]{0:T(512)(128)(4,1)S(1)} %compare_and_fusion), kind=kOutput, calls=%fused_computation.14 | convolution fusion | flops 3221356544 | bytes 6816256 | tf_op jit(solution)/shard_map/fpsc,cm->fpsm/dot_general | solution.py:39
  132.2 2.4 copy.25
  134.6 7.4 %all-to-all-start = ((f32[1,2,1024,256]{3,1,0,2:T(2,128)}), f32[1,2,1024,256]{3,1,0,2:T(2,128)S(1)}, u32[]{:S(2)}, u32[]{:S(2)}) async-start(f32[1,2,1024,256]{3,1,0,2:T(2,128)} %copy.25), calls=%async_computation | async-start | bytes 4194304 | tf_op jit(solution)/shard_map/all_to_all | solution.py:40
  142.0 0.0 all-reduce.4.cloned.1.call-start
  142.1 0.0 copy-done
  142.1 97.4 %gather_fusion = f32[16384]{0:T(1024)S(1)} fusion(f32[128]{0:T(128)S(1)} %copy-done, s32[16384]{0:T(1024)S(1)} %fusion.24), kind=kCustom, calls=%fused_computation | custom fusion | bytes 196608 | tf_op jit(solution)/shard_map/jit(_take)/gather | solution.py:20
  239.5 0.1 multiply_cosine_fusion
  239.6 0.0 all-to-all-done
  239.7 4.7 fusion.8
  244.3 0.0 copy-start.3
  244.3 0.0 copy-start.4
  244.3 4.0 fusion.2
  248.4 0.0 copy-done.3
  248.4 0.0 copy-done.4
  248.4 1.9 multiply_reduce_fusion
  250.3 1.9 fusion.38
  252.2 4.3 fusion.25
  256.5 2.3 fusion
  258.8 1.2 copy.29
  260.1 56.3 %all_to_all.33 = f32[32,2,32,256]{3,2,1,0:T(8,128)S(1)} all-to-all(f32[32,2,32,256]{3,2,1,0:T(8,128)S(1)} %copy.29), channel_id=1, replica_groups=mesh['tile'=8,'freq'=32] {'freq'}, dimensions={0} | all-to-all | bytes 4194304 | tf_op jit(solution)/shard_map/all_to_all | solution.py:50
  316.3 0.0 copy-start.1
  316.3 0.2 copy.30
  316.6 1.9 copy-done.1
  318.5 3.8 fusion.14
  322.4 0.2 copy.32
  322.6 4.7 scatter_custom_fusion
  327.3 0.0 copy-start.2
  327.3 0.0 all-reduce.4.cloned.1.call-update
  327.3 0.0 all-reduce.6.cloned.1.call-start
  327.3 150.7 %all-reduce.4.cloned.1.call-done = f32[2048,256]{1,0:T(8,128)} async-done(((f32[2048,256]{1,0:T(8,128)}), f32[2048,256]{1,0:T(8,128)}) %all-reduce.4.cloned.1.call-update) | async-done | bytes 2097168 | tf_op jit(solution)/shard_map/psum | solution.py:53
  478.0 0.0 all-reduce.6.cloned.1.call-update
  478.0 73.0 %all-reduce.6.cloned.1.call-done = f32[2048,256]{1,0:T(8,128)} async-done(((f32[2048,256]{1,0:T(8,128)}), f32[2048,256]{1,0:T(8,128)}) %all-reduce.6.cloned.1.call-update) | async-done | bytes 2097168 | tf_op jit(solution)/shard_map/psum | solution.py:53
  551.0 0.7 multiply_reduce_fusion.1
  551.7 78.6 %all-reduce = (f32[256]{0:T(256)S(1)}, f32[256]{0:T(256)S(1)}) all-reduce(f32[256]{0:T(256)S(1)} %get-tuple-element.8, f32[256]{0:T(256)S(1)} %multiply_reduce_fusion.1), channel_id=1, replica_groups=mesh['tile'=8,'freq'=32] {'tile','freq'}, use_global_device_ids=true, to_apply=%region_1.2 | all-reduce | flops 512 | bytes 4096 | tf_op jit(solution)/shard_map/psum | solution.py:46
  630.3 0.6 multiply_multiply_fusion
  630.9 0.0 copy-done.2
  630.9 1.3 multiply_subtract_fusion
  (4 shorter events, 0.1 us)
Async XLA Ops:
  7.2 134.9 %copy-start = (f32[128]{0:T(128)S(1)}, f32[128]{0:T(128)}, u32[]{:S(2)}) copy-start(f32[128]{0:T(128)} %param.9) | copy-start | bytes 1540
  7.2 112.9 %all-gather.2.cloned.1.call-start = ((), (), s32[]{:S(2)}) async-start(), calls=%async_computation.2 | async-start | bytes 2105344 | tf_op jit(solution)/shard_map/all_gather | solution.py:36
  134.6 105.1 %all-to-all-start = ((f32[1,2,1024,256]{3,1,0,2:T(2,128)}), f32[1,2,1024,256]{3,1,0,2:T(2,128)S(1)}, u32[]{:S(2)}, u32[]{:S(2)}) async-start(f32[1,2,1024,256]{3,1,0,2:T(2,128)} %copy.25), calls=%async_computation | async-start | bytes 4194304 | tf_op jit(solution)/shard_map/all_to_all | solution.py:40
  142.0 336.0 %all-reduce.4.cloned.1.call-start = ((), (), s32[]{:S(2)}) async-start(), calls=%async_computation.3 | async-start | bytes 4194304 | tf_op jit(solution)/shard_map/psum | solution.py:53
  244.3 4.1 copy-start.3
  244.3 4.1 copy-start.4
  316.3 2.2 copy-start.1
  327.3 303.6 %copy-start.2 = (f32[8,256]{1,0:T(8,128)S(1)}, f32[8,256]{1,0:T(8,128)}, u32[]{:S(2)}) copy-start(f32[8,256]{1,0:T(8,128)} %param.7) | copy-start | bytes 24580
  327.3 223.7 %all-reduce.6.cloned.1.call-start = ((), (), s32[]{:S(2)}) async-start(), calls=%async_computation.4 | async-start | bytes 4194304 | tf_op jit(solution)/shard_map/psum | solution.py:53
Sparse Core Ops, SparseCore 0:
  11.7 108.2 all-gather.1
  327.4 150.5 all-reduce.3
  480.4 70.5 all-reduce.5
